TPU v7x, 32 devices: a whole 2x2x4 slice. The times are simulated.
32 devices in a mesh: row: 8 (over z, x), col: 4 (over y, core).
Axes of the slice: x: 2, y: 2, z: 4, core: 2. Of those that a mesh axis runs over, the one named last changes fastest.
Arguments:
- diagonal: float32 [32, 512, 512], P(('row', 'col')), may hold values from -0.05 to 1.05
- lower: float32 [32, 512, 512], P(('row', 'col')), may hold values from -1 to 1, as said below
- upper: float32 [32, 512, 512], P(('row', 'col')), may hold values from -1 to 1, as said below
- right_side: float32 [32, 512, 128], P(('row', 'col')), may hold values from -6 to 6
- guess: float32 [32, 512, 128], P(('row', 'col')), may hold values from -4 to 4
Outputs:
- solution: float32 [32, 512, 128], P(('row', 'col'))
Inputs may be any that keep to these rules, and one draw needn't show every extreme that they name: `lower`: each block is one half of an orthogonal matrix. `upper`: each block is one half of an orthogonal matrix.
All inputs are finite; a program needn't handle non-finite values.
Results may differ from a plain program's by a relative error of at most 0.00026.
Values sent between devices are 32-bit elements; how exact they have to be, the bound alone decides.
A program may use at most 64 MiB of HBM per device.

v0:
```python
import jax
import jax.numpy as jnp
from jax import lax
from jax.sharding import PartitionSpec as P

AXES = ("row", "col")


def multiply(left, right):
    return jnp.dot(left, right, precision=lax.Precision.HIGH, preferred_element_type=jnp.float32)


def permuted(value, pairs, chain):
    kept = [(s, d) for s, d in pairs if 0 <= d < chain]
    return lax.ppermute(value, AXES, kept)


def first_step(matrix):
    order = matrix.shape[-1]
    eye = jnp.eye(order, dtype=jnp.float32)
    t = jnp.trace(matrix) / order
    return (2.0 * eye - matrix / t) / t, eye, t


def invert(matrix):
    approx, eye, _ = first_step(matrix)
    return multiply(approx, 2.0 * eye - multiply(matrix, approx))


def apply_inverse(matrix, value):
    t = jnp.trace(matrix) / matrix.shape[-1]

    def first(v):
        return (2.0 * v - multiply(matrix, v) / t) / t

    return first(2.0 * value - multiply(matrix, first(value)))


def body(diagonal, lower, upper, right_side, guess):
    chain = lax.axis_size("row") * lax.axis_size("col")
    place = lax.axis_index("row") * lax.axis_size("col") + lax.axis_index("col")
    even = place % 2 == 0
    diag, rhs, g = diagonal[0], right_side[0], guess[0]
    order = diag.shape[0]
    inward = jnp.where(even, upper[0], lower[0])
    edge = (place == 0) | (place == chain - 1)
    outward = jnp.where(edge, jnp.float32(0.0), jnp.where(even, lower[0], upper[0]))

    rows = range(chain)
    partner = [(i, i ^ 1) for i in rows]
    outer = [(i, i - 1 if i % 2 == 0 else i + 1) for i in rows]
    to_out = [(i, i - 2 if i % 2 == 0 else i + 2) for i in rows]
    to_in = [(i, i + 2 if i % 2 == 0 else i - 2) for i in rows]

    g_o = permuted(g, outer, chain)
    g_p = permuted(g, partner, chain)
    pivot = invert(diag)
    s_out = multiply(pivot, outward)
    so_o = permuted(s_out, outer, chain)
    s_in = multiply(pivot, inward)
    s_b = multiply(pivot, rhs)
    b_o, q_o = permuted((s_b, multiply(s_in, g_p)), outer, chain)
    si_p, so_p, b_p, h_p = permuted((s_in, s_out, s_b, multiply(s_out, g_o)), partner, chain)
    diag1 = diag - multiply(inward, si_p) - multiply(outward, so_o)
    rhs1 = rhs - multiply(inward, b_p) - multiply(outward, b_o)
    in1 = -multiply(inward, so_p)
    pivot = invert(diag1)
    h = multiply(pivot, outward)
    r_h = permuted(h, to_out, chain)
    r_g = permuted(multiply(si_p, multiply(pivot, in1)), to_in, chain)
    w_h = multiply(pivot, rhs1 + multiply(inward, h_p))
    w_g = multiply(si_p, multiply(pivot, rhs1 + multiply(outward, q_o)))
    r_wh = permuted(w_h, to_out, chain)
    r_wg = permuted(w_g, to_in, chain)
    diag2 = diag1 + multiply(multiply(in1, r_h), si_p) + multiply(outward, r_g)
    inner = rhs1 + multiply(outward, r_wg) - multiply(in1, r_wh)
    return apply_inverse(diag2, inner)[None]


def solution(mesh):
    spec = P(AXES, None, None)
    return jax.shard_map(body, mesh=mesh, in_specs=(spec,) * 5, out_specs=spec, check_vma=False)
```

profile of v0, /device:TPU:19, one launch (start us, length us, event | category | flops | bytes accessed | tf_op | source)
XLA Modules:
  0.0 136.0 jit_solution(5177465932543519197)
XLA Ops:
  0.0 3.8 %collective-permute-start.8 = (f32[512,128]{1,0:T(8,128)}, f32[512,128]{1,0:T(8,128)}, u32[]{:S(2)}, u32[]{:S(2)}) collective-permute-start(f32[512,128]{1,0:T(8,128)} %bitcast.95), channel_id=1, source_target_pairs={{1,2},{2,1},{3,4},{4,3},{5,6},{6,5},{7,8},{8,7},{9,10},{10,9},{11,... | collective-permute-start | bytes 786440 | tf_op jit(solution)/shard_map/ppermute | solution.py:15
  3.9 1.9 %fusion.27 = f32[]{:T(128)} fusion(f32[1,512,512]{2,1,0:T(8,128)} %param.5), kind=kLoop, calls=%fused_computation.43 | loop fusion | flops 786431 | bytes 1048580 | tf_op jit(solution)/shard_map/jit(trace)/reduce_sum | solution.py:21
  6.5 1.1 select_subtract_fusion.2
  7.6 1.0 fusion.10
  8.6 1.3 fusion.44
  9.9 3.5 %collective-permute-start.1 = (f32[512,128]{1,0:T(8,128)}, f32[512,128]{1,0:T(8,128)}, u32[]{:S(2)}, u32[]{:S(2)}) collective-permute-start(f32[512,128]{1,0:T(8,128)} %fusion.44), channel_id=1, source_target_pairs={{1,2},{2,1},{3,4},{4,3},{5,6},{6,5},{7,8},{8,7},{9,10},{10,9},{11,... | collective-permute-start | bytes 786440 | tf_op jit(solution)/shard_map/ppermute | solution.py:15
  13.4 0.1 collective-permute-start
  13.5 1.9 %select_select_fusion = (f32[1,512,512]{2,1,0:T(8,128)S(1)}, f32[1,512,512]{2,1,0:T(8,128)S(1)}) fusion(f32[1,512,512]{2,1,0:T(8,128)} %param.6, f32[1,512,512]{2,1,0:T(8,128)} %param.7, pred[]{:T(512)S(6)} %or.3, pred[]{:T(512)S(6)} %eq.40), kind=kLoop, calls=%fused_computation.52 | loop fusion | flops 786432 | bytes 4194306 | tf_op jit(solution)/shard_map/jit(_where)/select_n | solution.py:47
  15.4 2.0 %fusion.21 = f32[512,512]{1,0:T(8,128)} fusion(f32[512,512]{1,0:T(8,128)S(1)} %fusion.10, f32[1,512,512]{2,1,0:T(8,128)S(1)} %get-tuple-element.5), kind=kOutput, calls=%fused_computation.35 | convolution fusion | flops 805306368 | bytes 3145728 | tf_op jit(solution)/shard_map/dot_general | solution.py:10
  17.3 0.5 collective-permute-start.7
  17.8 1.0 fusion.31
  18.8 1.9 %collective-permute-done.1 = f32[512,128]{1,0:T(8,128)} collective-permute-done((f32[512,128]{1,0:T(8,128)}, f32[512,128]{1,0:T(8,128)}, u32[]{:S(2)}, u32[]{:S(2)}) %collective-permute-start.1) | collective-permute-done | bytes 262176 | tf_op jit(solution)/shard_map/ppermute | solution.py:15
  20.7 3.5 %collective-permute-start.3 = (f32[512,512]{1,0:T(8,128)}, f32[512,512]{1,0:T(8,128)S(1)}, u32[]{:S(2)}, u32[]{:S(2)}) collective-permute-start(f32[512,512]{1,0:T(8,128)} %fusion.21), channel_id=1, source_target_pairs={{1,2},{2,1},{3,4},{4,3},{5,6},{6,5},{7,8},{8,7},{9,10},{10,9},{11,... | collective-permute-start | bytes 3145736 | tf_op jit(solution)/shard_map/ppermute | solution.py:15
  24.2 1.5 %fusion.23 = f32[512,128]{1,0:T(8,128)S(1)} fusion(f32[512,128]{1,0:T(8,128)} %collective-permute-done.1, f32[1,512,512]{2,1,0:T(8,128)S(1)} %get-tuple-element.5), kind=kOutput, calls=%fused_computation.37 | convolution fusion | flops 201326592 | bytes 1572864 | tf_op jit(solution)/shard_map/dot_general | solution.py:10
  25.8 0.1 collective-permute-start.2
  25.8 1.8 %fusion.60 = f32[512,128]{1,0:T(8,128)S(1)} fusion(f32[512,512]{1,0:T(8,128)} %fusion.21, f32[512,128]{1,0:T(8,128)} %collective-permute-done.8), kind=kOutput, calls=%fused_computation.80 | convolution fusion | flops 201326592 | bytes 1572864 | tf_op jit(solution)/shard_map/dot_general | solution.py:10
  27.7 0.6 collective-permute-start.9
  28.3 0.6 fusion.57
  28.9 2.5 %collective-permute-start.5 = (f32[512,128]{1,0:T(8,128)S(1)}, f32[512,128]{1,0:T(8,128)S(1)}, u32[]{:S(2)}, u32[]{:S(2)}) collective-permute-start(f32[512,128]{1,0:T(8,128)S(1)} %fusion.57), channel_id=1, source_target_pairs={{1,2},{2,1},{3,4},{4,3},{5,6},{6,5},{7,8},{8,7},{9,10},{10,9},{11,... | collective-permute-start | bytes 786440 | tf_op jit(solution)/shard_map/ppermute | solution.py:15
  31.4 1.5 %fusion.8 = f32[512,128]{1,0:T(8,128)S(1)} fusion(f32[512,128]{1,0:T(8,128)S(1)} %fusion.23, f32[512,128]{1,0:T(8,128)} %collective-permute-done, f32[1,512,512]{2,1,0:T(8,128)S(1)} %get-tuple-element.6, f32[1,512,128]{2,1,0:T(8,128)S(1)} %copy-done.7), kind=kOutput, calls=%fused_computation.23 | convolution fusion | flops 201457664 | bytes 2097152 | tf_op jit(solution)/shard_map/dot_general | solution.py:10
  32.9 1.3 convolution_add_fusion.1
  34.2 18.8 %collective-permute-done.5 = f32[512,128]{1,0:T(8,128)S(1)} collective-permute-done((f32[512,128]{1,0:T(8,128)S(1)}, f32[512,128]{1,0:T(8,128)S(1)}, u32[]{:S(2)}, u32[]{:S(2)}) %collective-permute-start.5) | collective-permute-done | bytes 262176 | tf_op jit(solution)/shard_map/ppermute | solution.py:15
  53.0 1.3 convolution_add_fusion.3
  54.3 1.0 fusion.19
  55.4 0.2 copy-done.1
  55.5 2.6 %select_reduce_fusion.1 = (f32[]{:T(128)}, f32[512,512]{1,0:T(8,128)}) fusion(f32[512,512]{1,0:T(8,128)S(1)} %fusion.19, f32[512,512]{1,0:T(8,128)S(1)} %collective-permute-done.2, f32[1,512,512]{2,1,0:T(8,128)S(1)} %get-tuple-element.6, f32[1,512,512]{2,1,0:T(8,128)S(1)} %copy-done.1), kind=kOutput, calls=%fused_computation.51 | convolution fusion | flops 806617088 | bytes 5242884 | tf_op jit(solution)/shard_map/dot_general | solution.py:10
  58.7 2.7 %select_subtract_fusion = f32[512,512]{1,0:T(8,128)S(1)} fusion(f32[512,512]{1,0:T(8,128)} %get-tuple-element.8, f32[]{:T(128)S(6)} %div.65), kind=kOutput, calls=%fused_computation | convolution fusion | flops 807403520 | bytes 2097156 | tf_op jit(solution)/shard_map/dot_general | solution.py:10
  61.5 1.0 fusion.46
  62.5 0.6 fusion.61
  63.1 1.9 %collective-permute-start.10 = (f32[512,128]{1,0:T(8,128)S(1)}, f32[512,128]{1,0:T(8,128)S(1)}, u32[]{:S(2)}, u32[]{:S(2)}) collective-permute-start(f32[512,128]{1,0:T(8,128)S(1)} %fusion.61), channel_id=1, source_target_pairs={{1,3},{2,0},{3,5},{4,2},{5,7},{6,4},{7,9},{8,6},{9,11},{10,8},{11,... | collective-permute-start | bytes 786440 | tf_op jit(solution)/shard_map/ppermute | solution.py:15
  65.0 1.0 fusion.15
  66.1 2.2 %convolution_negate_fusion = f32[512,512]{1,0:T(8,128)S(1)} fusion(f32[512,512]{1,0:T(8,128)} %collective-permute-done.7, f32[1,512,512]{2,1,0:T(8,128)S(1)} %get-tuple-element.6), kind=kOutput, calls=%fused_computation.6 | convolution fusion | flops 805568512 | bytes 3145728 | tf_op jit(solution)/shard_map/dot_general | solution.py:10
  68.3 1.0 fusion.64
  69.3 1.0 fusion.65
  70.4 4.3 %collective-permute-start.12 = (f32[512,512]{1,0:T(8,128)S(1)}, f32[512,512]{1,0:T(8,128)S(1)}, u32[]{:S(2)}, u32[]{:S(2)}) collective-permute-start(f32[512,512]{1,0:T(8,128)S(1)} %fusion.65), channel_id=1, source_target_pairs={{0,2},{2,4},{3,1},{4,6},{5,3},{6,8},{7,5},{8,10},{9,7},{10,12},{11... | collective-permute-start | bytes 3145736 | tf_op jit(solution)/shard_map/ppermute | solution.py:15
  74.6 3.5 %collective-permute-start.11 = (f32[512,512]{1,0:T(8,128)S(1)}, f32[512,512]{1,0:T(8,128)S(1)}, u32[]{:S(2)}, u32[]{:S(2)}) collective-permute-start(f32[512,512]{1,0:T(8,128)S(1)} %fusion.15), channel_id=1, source_target_pairs={{1,3},{2,0},{3,5},{4,2},{5,7},{6,4},{7,9},{8,6},{9,11},{10,8},{11,... | collective-permute-start | bytes 3145736 | tf_op jit(solution)/shard_map/ppermute | solution.py:15
  78.2 0.6 fusion.58
  78.8 0.6 fusion.59
  79.4 2.9 %collective-permute-start.6 = (f32[512,128]{1,0:T(8,128)S(1)}, f32[512,128]{1,0:T(8,128)S(1)}, u32[]{:S(2)}, u32[]{:S(2)}) collective-permute-start(f32[512,128]{1,0:T(8,128)S(1)} %fusion.59), channel_id=1, source_target_pairs={{0,2},{2,4},{3,1},{4,6},{5,3},{6,8},{7,5},{8,10},{9,7},{10,12},{11... | collective-permute-start | bytes 786440 | tf_op jit(solution)/shard_map/ppermute | solution.py:15
  82.3 0.6 fusion.62
  82.9 44.9 %collective-permute-done.6 = f32[512,128]{1,0:T(8,128)S(1)} collective-permute-done((f32[512,128]{1,0:T(8,128)S(1)}, f32[512,128]{1,0:T(8,128)S(1)}, u32[]{:S(2)}, u32[]{:S(2)}) %collective-permute-start.6) | collective-permute-done | bytes 262176 | tf_op jit(solution)/shard_map/ppermute | solution.py:15
  127.7 1.3 fusion.7
  129.0 1.0 fusion.13
  130.1 1.0 fusion.63
  131.1 1.8 %select_reduce_fusion = (f32[]{:T(128)}, f32[512,512]{1,0:T(8,128)S(1)}) fusion(f32[512,512]{1,0:T(8,128)S(1)} %fusion.13, f32[512,512]{1,0:T(8,128)S(1)} %copy-done.2, f32[512,512]{1,0:T(8,128)S(1)} %fusion.63, f32[512,512]{1,0:T(8,128)S(1)} %collective-permute-done.2), kind=kOutput, calls=%fused_computation.50 | convolution fusion | flops 806617088 | bytes 5242884 | tf_op jit(solution)/shard_map/dot_general | solution.py:10
  133.5 0.6 fusion.6
  134.1 0.6 convolution_subtract_fusion.1
  134.7 1.3 fusion.4
  (26 shorter events, 0.1 us)
Async XLA Ops:
  0.0 6.5 %copy-start = (f32[1,512,512]{2,1,0:T(8,128)S(1)}, f32[1,512,512]{2,1,0:T(8,128)}, u32[]{:S(2)}) copy-start(f32[1,512,512]{2,1,0:T(8,128)} %param.5) | copy-start | bytes 3145732
  0.0 25.7 %collective-permute-start.8 = (f32[512,128]{1,0:T(8,128)}, f32[512,128]{1,0:T(8,128)}, u32[]{:S(2)}, u32[]{:S(2)}) collective-permute-start(f32[512,128]{1,0:T(8,128)} %bitcast.95), channel_id=1, source_target_pairs={{1,2},{2,1},{3,4},{4,3},{5,6},{6,5},{7,8},{8,7},{9,10},{10,9},{11,... | collective-permute-start | bytes 786440 | tf_op jit(solution)/shard_map/ppermute | solution.py:15
  3.8 23.9 %collective-permute-start.4 = (f32[512,128]{1,0:T(8,128)}, f32[512,128]{1,0:T(8,128)S(1)}, u32[]{:S(2)}, u32[]{:S(2)}) collective-permute-start(f32[512,128]{1,0:T(8,128)} %bitcast.96), channel_id=1, source_target_pairs={{0,1},{1,0},{2,3},{3,2},{4,5},{5,4},{6,7},{7,6},{8,9},{9,8},{10,11... | collective-permute-start | bytes 786440 | tf_op jit(solution)/shard_map/ppermute | solution.py:15
  7.6 1.0 copy-start.6
  9.9 10.8 %collective-permute-start.1 = (f32[512,128]{1,0:T(8,128)}, f32[512,128]{1,0:T(8,128)}, u32[]{:S(2)}, u32[]{:S(2)}) collective-permute-start(f32[512,128]{1,0:T(8,128)} %fusion.44), channel_id=1, source_target_pairs={{1,2},{2,1},{3,4},{4,3},{5,6},{6,5},{7,8},{8,7},{9,10},{10,9},{11,... | collective-permute-start | bytes 786440 | tf_op jit(solution)/shard_map/ppermute | solution.py:15
  13.4 15.5 %collective-permute-start = (f32[512,128]{1,0:T(8,128)}, f32[512,128]{1,0:T(8,128)}, u32[]{:S(2)}, u32[]{:S(2)}) collective-permute-start(f32[512,128]{1,0:T(8,128)} %fusion.44), channel_id=1, source_target_pairs={{0,1},{1,0},{2,3},{3,2},{4,5},{5,4},{6,7},{7,6},{8,9},{9,8},{10,11... | collective-permute-start | bytes 786440 | tf_op jit(solution)/shard_map/ppermute | solution.py:15
  17.3 48.7 %collective-permute-start.7 = (f32[512,512]{1,0:T(8,128)}, f32[512,512]{1,0:T(8,128)}, u32[]{:S(2)}, u32[]{:S(2)}) collective-permute-start(f32[512,512]{1,0:T(8,128)} %fusion.21), channel_id=1, source_target_pairs={{0,1},{1,0},{2,3},{3,2},{4,5},{5,4},{6,7},{7,6},{8,9},{9,8},{10,11... | collective-permute-start | bytes 3145736 | tf_op jit(solution)/shard_map/ppermute | solution.py:15
  20.7 33.6 %collective-permute-start.3 = (f32[512,512]{1,0:T(8,128)}, f32[512,512]{1,0:T(8,128)S(1)}, u32[]{:S(2)}, u32[]{:S(2)}) collective-permute-start(f32[512,512]{1,0:T(8,128)} %fusion.21), channel_id=1, source_target_pairs={{1,2},{2,1},{3,4},{4,3},{5,6},{6,5},{7,8},{8,7},{9,10},{10,9},{11,... | collective-permute-start | bytes 3145736 | tf_op jit(solution)/shard_map/ppermute | solution.py:15
  25.8 29.6 %collective-permute-start.2 = (f32[512,512]{1,0:T(8,128)S(1)}, f32[512,512]{1,0:T(8,128)S(1)}, u32[]{:S(2)}, u32[]{:S(2)}) collective-permute-start(f32[512,512]{1,0:T(8,128)S(1)} %fusion.31), channel_id=1, source_target_pairs={{0,1},{1,0},{2,3},{3,2},{4,5},{5,4},{6,7},{7,6},{8,9},{9,8},{10,11... | collective-permute-start | bytes 3145736 | tf_op jit(solution)/shard_map/ppermute | solution.py:15
  27.7 3.7 %copy-start.7 = (f32[1,512,128]{2,1,0:T(8,128)S(1)}, f32[1,512,128]{2,1,0:T(8,128)}, u32[]{:S(2)}) copy-start(f32[1,512,128]{2,1,0:T(8,128)} %param.8) | copy-start | bytes 786436
  27.7 5.2 %collective-permute-start.9 = (f32[512,128]{1,0:T(8,128)S(1)}, f32[512,128]{1,0:T(8,128)S(1)}, u32[]{:S(2)}, u32[]{:S(2)}) collective-permute-start(f32[512,128]{1,0:T(8,128)S(1)} %fusion.60), channel_id=1, source_target_pairs={{0,1},{1,0},{2,3},{3,2},{4,5},{5,4},{6,7},{7,6},{8,9},{9,8},{10,11... | collective-permute-start | bytes 786440 | tf_op jit(solution)/shard_map/ppermute | solution.py:15
  28.9 24.1 %collective-permute-start.5 = (f32[512,128]{1,0:T(8,128)S(1)}, f32[512,128]{1,0:T(8,128)S(1)}, u32[]{:S(2)}, u32[]{:S(2)}) collective-permute-start(f32[512,128]{1,0:T(8,128)S(1)} %fusion.57), channel_id=1, source_target_pairs={{1,2},{2,1},{3,4},{4,3},{5,6},{6,5},{7,8},{8,7},{9,10},{10,9},{11,... | collective-permute-start | bytes 786440 | tf_op jit(solution)/shard_map/ppermute | solution.py:15
  54.3 1.2 copy-start.1
  58.7 2.7 %copy-start.2 = (f32[512,512]{1,0:T(8,128)S(1)}, f32[512,512]{1,0:T(8,128)}, u32[]{:S(2)}) copy-start(f32[512,512]{1,0:T(8,128)} %get-tuple-element.8) | copy-start | bytes 3145732
  61.4 1.1 copy-start.4
  63.1 19.1 %collective-permute-start.10 = (f32[512,128]{1,0:T(8,128)S(1)}, f32[512,128]{1,0:T(8,128)S(1)}, u32[]{:S(2)}, u32[]{:S(2)}) collective-permute-start(f32[512,128]{1,0:T(8,128)S(1)} %fusion.61), channel_id=1, source_target_pairs={{1,3},{2,0},{3,5},{4,2},{5,7},{6,4},{7,9},{8,6},{9,11},{10,8},{11,... | collective-permute-start | bytes 786440 | tf_op jit(solution)/shard_map/ppermute | solution.py:15
  69.3 8.8 %copy-start.3 = (f32[512,128]{1,0:T(8,128)S(1)}, f32[512,128]{1,0:T(8,128)}, u32[]{:S(2)}) copy-start(f32[512,128]{1,0:T(8,128)} %convolution_add_fusion.3) | copy-start | bytes 786436
  70.4 58.7 %collective-permute-start.12 = (f32[512,512]{1,0:T(8,128)S(1)}, f32[512,512]{1,0:T(8,128)S(1)}, u32[]{:S(2)}, u32[]{:S(2)}) collective-permute-start(f32[512,512]{1,0:T(8,128)S(1)} %fusion.65), channel_id=1, source_target_pairs={{0,2},{2,4},{3,1},{4,6},{5,3},{6,8},{7,5},{8,10},{9,7},{10,12},{11... | collective-permute-start | bytes 3145736 | tf_op jit(solution)/shard_map/ppermute | solution.py:15
  74.6 55.4 %collective-permute-start.11 = (f32[512,512]{1,0:T(8,128)S(1)}, f32[512,512]{1,0:T(8,128)S(1)}, u32[]{:S(2)}, u32[]{:S(2)}) collective-permute-start(f32[512,512]{1,0:T(8,128)S(1)} %fusion.15), channel_id=1, source_target_pairs={{1,3},{2,0},{3,5},{4,2},{5,7},{6,4},{7,9},{8,6},{9,11},{10,8},{11,... | collective-permute-start | bytes 3145736 | tf_op jit(solution)/shard_map/ppermute | solution.py:15
  79.4 48.4 %collective-permute-start.6 = (f32[512,128]{1,0:T(8,128)S(1)}, f32[512,128]{1,0:T(8,128)S(1)}, u32[]{:S(2)}, u32[]{:S(2)}) collective-permute-start(f32[512,128]{1,0:T(8,128)S(1)} %fusion.59), channel_id=1, source_target_pairs={{0,2},{2,4},{3,1},{4,6},{5,3},{6,8},{7,5},{8,10},{9,7},{10,12},{11... | collective-permute-start | bytes 786440 | tf_op jit(solution)/shard_map/ppermute | solution.py:15
  131.1 2.4 %copy-start.5 = (f32[512,128]{1,0:T(8,128)S(1)}, f32[512,128]{1,0:T(8,128)}, u32[]{:S(2)}) copy-start(f32[512,128]{1,0:T(8,128)} %fusion.7) | copy-start | bytes 786436
where the time goes:
time: 137 us; the launch traced here: 136 us
  waiting for transfers between devices  65.6 us (48%)
  matrix products  37.1 us (27%)
  starting transfers between devices  27.1 us (20%)
  other arithmetic  3.75 us (3%)
  between operations  2.28 us (2%)
    ppermute x13, waiting for transfers between devices, permuted(): return lax.ppermute(value, AXES, kept)  65.6 us
    dot_general x30, matrix products, multiply(): jnp.dot(left, right, precision=lax.Precision.HIGH, preferred_element_type...  37.1 us
    ppermute x13, starting transfers between devices, permuted(): return lax.ppermute(value, AXES, kept)  27.1 us
  transfers between devices with their start and end apart: 13, of which 3 were waited for; matrix products, arithmetic and copies ran while one was open for 26% of the time, Pallas kernels for 0%

commit v1 on v0

v1 whole, which is shorter than its diff:
```python
import functools
from collections import namedtuple

import jax
import jax.numpy as jnp
from jax import lax
from jax.experimental import pallas as pl
from jax.experimental.pallas import tpu as pltpu
from jax.sharding import PartitionSpec as P

AXES = ("row", "col")
F32, BF16 = jnp.float32, jnp.bfloat16
CHUNKS = 2

MESSAGES = (
    ("g_outer", 1), ("g_partner", 1),
    ("so_outer", CHUNKS), ("so_partner", CHUNKS), ("si_partner", CHUNKS),
    ("b_outer", 1), ("b_partner", 1), ("q_outer", 1), ("v_partner", 1),
    ("h_out", CHUNKS), ("wh_out", 1), ("g_in", CHUNKS), ("wg_in", 1),
)
FIRST = {}
for _name, _count in MESSAGES:
    FIRST[_name] = sum(count for _, count in MESSAGES[: len(FIRST)])
TOTAL = sum(count for _, count in MESSAGES)


def scratch_types(order, columns):
    matrix = pltpu.VMEM((order, order), F32)
    chunked = pltpu.VMEM((CHUNKS, order, order // CHUNKS), F32)
    vector = pltpu.VMEM((order, columns), F32)
    pair = pltpu.VMEM((2, order, order), BF16)
    vector_pair = pltpu.VMEM((2, order, columns), BF16)
    types = dict(diag=matrix, l_in=matrix, l_out=matrix, rhs=vector)
    types.update({name: chunked for name in ("s_out", "s_in", "h_mat", "g_mat")})
    types.update({name: vector for name in ("s_b", "q_vec", "v_vec", "wh", "wg", "via")})
    types.update({f"r_{name}": chunked if count > 1 else vector for name, count in MESSAGES})
    types.update({name: pair for name in ("d2", "x2", "y2", "p2", "lin2", "lout2", "sin2", "sout2", "sip2", "in2", "t2", "u2", "k2")})
    types.update(vec2=vector_pair)
    types.update(load_sem=pltpu.SemaphoreType.DMA((4,)))
    types.update(send_sem=pltpu.SemaphoreType.DMA((TOTAL,)), recv_sem=pltpu.SemaphoreType.DMA((TOTAL,)))
    return types


def kernel(chain, across, names, d_hbm, low_hbm, up_hbm, b_hbm, g_hbm, out_ref, *scratch):
    s = namedtuple("Scratch", names)(*scratch)
    order = s.diag.shape[0]
    width = order // CHUNKS
    place = lax.axis_index("row") * across + lax.axis_index("col")
    odd = lax.rem(place, 2)
    even = odd == 0
    step = 1 - 2 * odd
    inside = (place > 0) & (place < chain - 1)
    edge = (place == 0) | (place == chain - 1)
    deep = (place != 1) & (place != chain - 2)
    shallow = (place == 1) | (place == chain - 2)

    def device(offset):
        index = lax.rem(place + offset * step + chain, chain)
        return (index // across, lax.rem(index, across))

    peers = {"partner": device(1), "outer": device(-1), "out": device(-2), "in": device(2)}
    sent_if = {"partner": None, "outer": inside, "out": inside, "in": deep}
    came_if = {"partner": None, "outer": inside, "out": deep, "in": inside}

    def guarded(condition, action):
        if condition is None:
            action()
        else:
            pl.when(condition)(action)

    def copy(name, src, chunk):
        dst = getattr(s, "r_" + name)
        index = FIRST[name] + chunk
        if dst.ndim == 3:
            dst = dst.at[chunk]
        return pltpu.make_async_remote_copy(
            src_ref=src if src is not None else dst,
            dst_ref=dst,
            send_sem=s.send_sem.at[index],
            recv_sem=s.recv_sem.at[index],
            device_id=peers[name.split("_")[1]],
            device_id_type=pl.DeviceIdType.MESH,
        )

    pending = []

    def send(name, src, chunk=0):
        guarded(sent_if[name.split("_")[1]], lambda: copy(name, src, chunk).start())
        pending.append((name, src, chunk))

    def receive(name, chunk=0):
        guarded(came_if[name.split("_")[1]], lambda: copy(name, None, chunk).wait_recv())

    def load(src, dst, index):
        return pltpu.make_async_copy(src.at[0], dst, s.load_sem.at[index])

    def load_out(act):
        pl.when(inside & even)(lambda: act(load(low_hbm, s.l_out, 1)))
        pl.when(inside & (odd == 1))(lambda: act(load(up_hbm, s.l_out, 1)))

    def load_in(act):
        pl.when(even)(lambda: act(load(up_hbm, s.l_in, 2)))
        pl.when(odd == 1)(lambda: act(load(low_hbm, s.l_in, 2)))

    load(d_hbm, s.diag, 0).start()
    load_out(lambda c: c.start())
    load_in(lambda c: c.start())
    load(b_hbm, s.rhs, 3).start()

    barrier = pltpu.get_barrier_semaphore()
    for side in ("partner", "outer", "out", "in"):
        guarded(sent_if[side], lambda: pl.semaphore_signal(
            barrier, inc=1, device_id=peers[side], device_id_type=pl.DeviceIdType.MESH))
    pl.semaphore_wait(barrier, 1 + jnp.where(inside, 2, 0) + jnp.where(deep, 1, 0))

    send("g_outer", g_hbm.at[0])
    send("g_partner", g_hbm.at[0])

    def zero(*refs):
        for ref in refs:
            ref[...] = jnp.zeros_like(ref)

    pl.when(edge)(lambda: zero(s.l_out, s.r_g_outer, s.r_so_outer, s.r_b_outer, s.r_q_outer, s.r_g_in, s.r_wg_in))
    pl.when(shallow)(lambda: zero(s.r_h_out, s.r_wh_out))

    def cols(chunk):
        return slice(chunk * width, (chunk + 1) * width)

    def put(pair, value, where=slice(None)):
        high = value.astype(BF16)
        pair[0, :, where] = high
        pair[1, :, where] = (value - high.astype(F32)).astype(BF16)

    def dot(left, right):
        return jnp.dot(left, right, preferred_element_type=F32)

    def multiply(left, right, where=slice(None)):
        high, low = right[0, :, where], right[1, :, where]
        return dot(left[0], high) + (dot(left[0], low) + dot(left[1], high))

    def eye(chunk):
        rows = lax.broadcasted_iota(jnp.int32, (order, width), 0)
        return (rows == lax.broadcasted_iota(jnp.int32, (order, width), 1) + chunk * width).astype(F32)

    def mean_diag():
        total = jnp.float32(0.0)
        for c in range(CHUNKS):
            total += jnp.sum(eye(c) * s.diag[:, cols(c)])
        return total / order

    def invert():
        scale = 1.0 / mean_diag()
        for c in range(CHUNKS):
            block = s.diag[:, cols(c)]
            put(s.d2, block, cols(c))
            put(s.x2, (2.0 * eye(c) - block * scale) * scale, cols(c))
        for c in range(CHUNKS):
            put(s.y2, 2.0 * eye(c) - multiply(s.d2, s.x2, cols(c)), cols(c))
        for c in range(CHUNKS):
            put(s.p2, multiply(s.x2, s.y2, cols(c)), cols(c))

    def times(left, vector):
        put(s.vec2, vector)
        return multiply(left, s.vec2)

    load(d_hbm, s.diag, 0).wait()
    invert()
    load_out(lambda c: c.wait())
    put(s.lout2, s.l_out[...])
    for c in range(CHUNKS):
        block = multiply(s.p2, s.lout2, cols(c))
        s.s_out[c] = block
        send("so_outer", s.s_out.at[c], c)
        send("so_partner", s.s_out.at[c], c)
        put(s.sout2, block, cols(c))
    load(b_hbm, s.rhs, 3).wait()
    s.s_b[...] = times(s.p2, s.rhs[...])
    send("b_outer", s.s_b)
    send("b_partner", s.s_b)
    load_in(lambda c: c.wait())
    put(s.lin2, s.l_in[...])
    for c in range(CHUNKS):
        block = multiply(s.p2, s.lin2, cols(c))
        s.s_in[c] = block
        send("si_partner", s.s_in.at[c], c)
        put(s.sin2, block, cols(c))
    receive("g_partner")
    s.q_vec[...] = times(s.sin2, s.r_g_partner[...])
    send("q_outer", s.q_vec)
    receive("g_outer")
    s.v_vec[...] = times(s.sout2, s.r_g_outer[...])
    send("v_partner", s.v_vec)

    for c in range(CHUNKS):
        receive("si_partner", c)
        put(s.sip2, s.r_si_partner[c], cols(c))
        s.diag[:, cols(c)] = s.diag[:, cols(c)] - multiply(s.lin2, s.sip2, cols(c))
    for c in range(CHUNKS):
        receive("so_partner", c)
        put(s.t2, s.r_so_partner[c], cols(c))
        put(s.in2, -multiply(s.lin2, s.t2, cols(c)), cols(c))
    receive("b_partner")
    s.rhs[...] = s.rhs[...] - times(s.lin2, s.r_b_partner[...])
    receive("v_partner")
    s.via[...] = times(s.lin2, s.r_v_partner[...])
    for c in range(CHUNKS):
        receive("so_outer", c)
        put(s.u2, s.r_so_outer[c], cols(c))
        s.diag[:, cols(c)] = s.diag[:, cols(c)] - multiply(s.lout2, s.u2, cols(c))

    invert()
    for c in range(CHUNKS):
        s.h_mat[c] = multiply(s.p2, s.lout2, cols(c))
        send("h_out", s.h_mat.at[c], c)
    receive("b_outer")
    s.rhs[...] = s.rhs[...] - times(s.lout2, s.r_b_outer[...])
    s.wh[...] = times(s.p2, s.rhs[...] + s.via[...])
    send("wh_out", s.wh)
    for c in range(CHUNKS):
        put(s.k2, multiply(s.sip2, s.p2, cols(c)), cols(c))
    for c in range(CHUNKS):
        s.g_mat[c] = multiply(s.k2, s.in2, cols(c))
        send("g_in", s.g_mat.at[c], c)
    receive("q_outer")
    s.wg[...] = times(s.k2, s.rhs[...] + times(s.lout2, s.r_q_outer[...]))
    send("wg_in", s.wg)

    for c in range(CHUNKS):
        receive("h_out", c)
        put(s.t2, s.r_h_out[c], cols(c))
        put(s.u2, multiply(s.in2, s.t2, cols(c)), cols(c))
    for c in range(CHUNKS):
        s.diag[:, cols(c)] = s.diag[:, cols(c)] + multiply(s.u2, s.sip2, cols(c))
    receive("wh_out")
    s.rhs[...] = s.rhs[...] - times(s.in2, s.r_wh_out[...])
    for c in range(CHUNKS):
        receive("g_in", c)
        put(s.t2, s.r_g_in[c], cols(c))
        block = s.diag[:, cols(c)] + multiply(s.lout2, s.t2, cols(c))
        s.diag[:, cols(c)] = block
        put(s.d2, block, cols(c))
    scale = 1.0 / mean_diag()
    receive("wg_in")
    inner = s.rhs[...] + times(s.lout2, s.r_wg_in[...])

    half = (2.0 * inner - times(s.d2, inner) * scale) * scale
    rest = 2.0 * inner - times(s.d2, half)
    out_ref[...] = (2.0 * rest - times(s.d2, rest) * scale) * scale

    for name, src, chunk in pending:
        guarded(sent_if[name.split("_")[1]], lambda: copy(name, src, chunk).wait_send())


def body(diagonal, lower, upper, right_side, guess):
    across = lax.axis_size("col")
    chain = lax.axis_size("row") * across
    order, columns = right_side.shape[1:]
    types = scratch_types(order, columns)
    result = pl.pallas_call(
        functools.partial(kernel, chain, across, tuple(types)),
        out_shape=jax.ShapeDtypeStruct((order, columns), F32),
        in_specs=[pl.BlockSpec(memory_space=pl.ANY)] * 5,
        out_specs=pl.BlockSpec(memory_space=pltpu.VMEM),
        scratch_shapes=list(types.values()),
        compiler_params=pltpu.CompilerParams(collective_id=0, has_side_effects=True),
    )(diagonal, lower, upper, right_side, guess)
    return result[None]


def solution(mesh):
    spec = P(AXES, None, None)
    return jax.shard_map(body, mesh=mesh, in_specs=(spec,) * 5, out_specs=spec, check_vma=False)
```

time: 137 us -> 112 us (0.82)
  the two profiles are of different devices: /device:TPU:19 before, /device:TPU:29 now
where the time goes in v1:
time: 112 us
  Pallas kernels  111 us (99%)
  local copies, waits for them, and re-layouts  1.67 us (1%)
    pallas_call x1, Pallas kernels, body(): pl.pallas_call(functools.partial(kernel, chain, across, tuple(types)), ou...  111 us

profile of v1, /device:TPU:29, one launch (start us, length us, event | category | flops | bytes accessed | tf_op | source)
XLA Modules:
  0.0 112.2 jit_solution(18309134374992793983)
XLA Ops:
  0.0 110.5 %shard_map.55 = f32[512,128]{1,0:T(8,128)} custom-call(f32[1,512,512]{2,1,0:T(8,128)} %d_hbm.1, f32[1,512,512]{2,1,0:T(8,128)} %low_hbm.1, f32[1,512,512]{2,1,0:T(8,128)} %up_hbm.1, f32[1,512,128]{2,1,0:T(8,128)} %b_hbm.1, f32[1,512,128]{2,1,0:T(8,128)} %g_hbm.1), custom_call_target="tpu_custom_call" | custom-call | tf_op jit(solution)/shard_map/pallas_call | solution.py:259
  110.5 1.7 %copy.7 = f32[1,512,128]{2,1,0:T(8,128)} copy(f32[1,512,128]{2,1,0:T(8,128)} %bitcast.1) | data formatting | bytes 524288

commit v2 on v1

--- a/solution.py
+++ b/solution.py
@@ -15,7 +15,7 @@
 MESSAGES = (
     ("g_outer", 1), ("g_partner", 1),
     ("so_outer", CHUNKS), ("so_partner", CHUNKS), ("si_partner", CHUNKS),
-    ("b_outer", 1), ("b_partner", 1), ("q_outer", 1), ("v_partner", 1),
+    ("b_partner", 1), ("e_outer", 1), ("v_partner", 1),
     ("h_out", CHUNKS), ("wh_out", 1), ("g_in", CHUNKS), ("wg_in", 1),
 )
 FIRST = {}
@@ -32,10 +32,10 @@
     vector_pair = pltpu.VMEM((2, order, columns), BF16)
     types = dict(diag=matrix, l_in=matrix, l_out=matrix, rhs=vector)
     types.update({name: chunked for name in ("s_out", "s_in", "h_mat", "g_mat")})
-    types.update({name: vector for name in ("s_b", "q_vec", "v_vec", "wh", "wg", "via")})
+    types.update({name: vector for name in ("s_b", "e_vec", "v_vec", "wh", "wg", "via")})
     types.update({f"r_{name}": chunked if count > 1 else vector for name, count in MESSAGES})
     types.update({name: pair for name in ("d2", "x2", "y2", "p2", "lin2", "lout2", "sin2", "sout2", "sip2", "in2", "t2", "u2", "k2")})
-    types.update(vec2=vector_pair)
+    types.update(vec2=vector_pair, bp2=vector_pair)
     types.update(load_sem=pltpu.SemaphoreType.DMA((4,)))
     types.update(send_sem=pltpu.SemaphoreType.DMA((TOTAL,)), recv_sem=pltpu.SemaphoreType.DMA((TOTAL,)))
     return types
@@ -120,7 +120,7 @@
         for ref in refs:
             ref[...] = jnp.zeros_like(ref)
 
-    pl.when(edge)(lambda: zero(s.l_out, s.r_g_outer, s.r_so_outer, s.r_b_outer, s.r_q_outer, s.r_g_in, s.r_wg_in))
+    pl.when(edge)(lambda: zero(s.l_out, s.r_g_outer, s.r_so_outer, s.r_e_outer, s.r_g_in, s.r_wg_in))
     pl.when(shallow)(lambda: zero(s.r_h_out, s.r_wh_out))
 
     def cols(chunk):
@@ -175,7 +175,6 @@
         put(s.sout2, block, cols(c))
     load(b_hbm, s.rhs, 3).wait()
     s.s_b[...] = times(s.p2, s.rhs[...])
-    send("b_outer", s.s_b)
     send("b_partner", s.s_b)
     load_in(lambda c: c.wait())
     put(s.lin2, s.l_in[...])
@@ -185,8 +184,8 @@
         send("si_partner", s.s_in.at[c], c)
         put(s.sin2, block, cols(c))
     receive("g_partner")
-    s.q_vec[...] = times(s.sin2, s.r_g_partner[...])
-    send("q_outer", s.q_vec)
+    s.e_vec[...] = s.s_b[...] - times(s.sin2, s.r_g_partner[...])
+    send("e_outer", s.e_vec)
     receive("g_outer")
     s.v_vec[...] = times(s.sout2, s.r_g_outer[...])
     send("v_partner", s.v_vec)
@@ -200,7 +199,8 @@
         put(s.t2, s.r_so_partner[c], cols(c))
         put(s.in2, -multiply(s.lin2, s.t2, cols(c)), cols(c))
     receive("b_partner")
-    s.rhs[...] = s.rhs[...] - times(s.lin2, s.r_b_partner[...])
+    put(s.bp2, s.r_b_partner[...])
+    s.rhs[...] = s.rhs[...] - multiply(s.lin2, s.bp2)
     receive("v_partner")
     s.via[...] = times(s.lin2, s.r_v_partner[...])
     for c in range(CHUNKS):
@@ -212,8 +212,6 @@
     for c in range(CHUNKS):
         s.h_mat[c] = multiply(s.p2, s.lout2, cols(c))
         send("h_out", s.h_mat.at[c], c)
-    receive("b_outer")
-    s.rhs[...] = s.rhs[...] - times(s.lout2, s.r_b_outer[...])
     s.wh[...] = times(s.p2, s.rhs[...] + s.via[...])
     send("wh_out", s.wh)
     for c in range(CHUNKS):
@@ -221,8 +219,8 @@
     for c in range(CHUNKS):
         s.g_mat[c] = multiply(s.k2, s.in2, cols(c))
         send("g_in", s.g_mat.at[c], c)
-    receive("q_outer")
-    s.wg[...] = times(s.k2, s.rhs[...] + times(s.lout2, s.r_q_outer[...]))
+    receive("e_outer")
+    s.wg[...] = times(s.k2, s.rhs[...] - times(s.lout2, s.r_e_outer[...])) - s.r_b_partner[...]
     send("wg_in", s.wg)
 
     for c in range(CHUNKS):
@@ -232,7 +230,7 @@
     for c in range(CHUNKS):
         s.diag[:, cols(c)] = s.diag[:, cols(c)] + multiply(s.u2, s.sip2, cols(c))
     receive("wh_out")
-    s.rhs[...] = s.rhs[...] - times(s.in2, s.r_wh_out[...])
+    s.rhs[...] = s.rhs[...] - times(s.in2, s.r_wh_out[...] - multiply(s.t2, s.bp2))
     for c in range(CHUNKS):
         receive("g_in", c)
         put(s.t2, s.r_g_in[c], cols(c))

time: 112 us -> 105 us (0.938)
  Pallas kernels: 111 us -> 103 us
    pallas_call x1, Pallas kernels: 111 us -> 103 us  [body(): pl.pallas_call(functools.partial(kernel, chain, across, tuple(types)), ou...]
where the time goes in v2:
time: 105 us; the launch traced here: 104 us
  Pallas kernels  103 us (98%)
  local copies, waits for them, and re-layouts  1.67 us (2%)
    pallas_call x1, Pallas kernels, body(): pl.pallas_call(functools.partial(kernel, chain, across, tuple(types)), ou...  103 us

profile of v2, /device:TPU:29, one launch (start us, length us, event | category | flops | bytes accessed | tf_op | source)
XLA Modules:
  0.0 104.3 jit_solution(12271215722479348458)
XLA Ops:
  0.0 102.7 %shard_map.55 = f32[512,128]{1,0:T(8,128)} custom-call(f32[1,512,512]{2,1,0:T(8,128)} %d_hbm.1, f32[1,512,512]{2,1,0:T(8,128)} %low_hbm.1, f32[1,512,512]{2,1,0:T(8,128)} %up_hbm.1, f32[1,512,128]{2,1,0:T(8,128)} %b_hbm.1, f32[1,512,128]{2,1,0:T(8,128)} %g_hbm.1), custom_call_target="tpu_custom_call" | custom-call | tf_op jit(solution)/shard_map/pallas_call | solution.py:257
  102.7 1.7 %copy.7 = f32[1,512,128]{2,1,0:T(8,128)} copy(f32[1,512,128]{2,1,0:T(8,128)} %bitcast.1) | data formatting | bytes 524288

commit v3 on v2

--- a/solution.py
+++ b/solution.py
@@ -102,15 +102,15 @@
         pl.when(even)(lambda: act(load(up_hbm, s.l_in, 2)))
         pl.when(odd == 1)(lambda: act(load(low_hbm, s.l_in, 2)))
 
+    barrier = pltpu.get_barrier_semaphore()
+    for side in ("partner", "outer", "out", "in"):
+        guarded(sent_if[side], lambda: pl.semaphore_signal(
+            barrier, inc=1, device_id=peers[side], device_id_type=pl.DeviceIdType.MESH))
     load(d_hbm, s.diag, 0).start()
     load_out(lambda c: c.start())
     load_in(lambda c: c.start())
     load(b_hbm, s.rhs, 3).start()
 
-    barrier = pltpu.get_barrier_semaphore()
-    for side in ("partner", "outer", "out", "in"):
-        guarded(sent_if[side], lambda: pl.semaphore_signal(
-            barrier, inc=1, device_id=peers[side], device_id_type=pl.DeviceIdType.MESH))
     pl.semaphore_wait(barrier, 1 + jnp.where(inside, 2, 0) + jnp.where(deep, 1, 0))
 
     send("g_outer", g_hbm.at[0])
@@ -234,16 +234,10 @@
     for c in range(CHUNKS):
         receive("g_in", c)
         put(s.t2, s.r_g_in[c], cols(c))
-        block = s.diag[:, cols(c)] + multiply(s.lout2, s.t2, cols(c))
-        s.diag[:, cols(c)] = block
-        put(s.d2, block, cols(c))
-    scale = 1.0 / mean_diag()
+        s.diag[:, cols(c)] = s.diag[:, cols(c)] + multiply(s.lout2, s.t2, cols(c))
+    invert()
     receive("wg_in")
-    inner = s.rhs[...] + times(s.lout2, s.r_wg_in[...])
-
-    half = (2.0 * inner - times(s.d2, inner) * scale) * scale
-    rest = 2.0 * inner - times(s.d2, half)
-    out_ref[...] = (2.0 * rest - times(s.d2, rest) * scale) * scale
+    out_ref[...] = times(s.p2, s.rhs[...] + times(s.lout2, s.r_wg_in[...]))
 
     for name, src, chunk in pending:
         guarded(sent_if[name.split("_")[1]], lambda: copy(name, src, chunk).wait_send())

time: 105 us -> 105 us (level)
  no operation moved by 1% of the time
where the time goes in v3:
time: 105 us
  Pallas kernels  103 us (98%)
  local copies, waits for them, and re-layouts  1.67 us (2%)
    pallas_call x1, Pallas kernels, body(): pl.pallas_call(functools.partial(kernel, chain, across, tuple(types)), ou...  103 us

profile of v3, /device:TPU:29, one launch (start us, length us, event | category | flops | bytes accessed | tf_op | source)
XLA Modules:
  0.0 104.5 jit_solution(17722976663667170161)
XLA Ops:
  0.0 102.8 %shard_map.55 = f32[512,128]{1,0:T(8,128)} custom-call(f32[1,512,512]{2,1,0:T(8,128)} %d_hbm.1, f32[1,512,512]{2,1,0:T(8,128)} %low_hbm.1, f32[1,512,512]{2,1,0:T(8,128)} %up_hbm.1, f32[1,512,128]{2,1,0:T(8,128)} %b_hbm.1, f32[1,512,128]{2,1,0:T(8,128)} %g_hbm.1), custom_call_target="tpu_custom_call" | custom-call | tf_op jit(solution)/shard_map/pallas_call | solution.py:251
  102.9 1.7 %copy.7 = f32[1,512,128]{2,1,0:T(8,128)} copy(f32[1,512,128]{2,1,0:T(8,128)} %bitcast.1) | data formatting | bytes 524288
